TPU v7x, 128 devices: a whole 4x4x4 slice. The times are simulated.
128 devices in a mesh: grid: 16 (over y, z), blk: 8 (over x, core).
Axes of the slice: x: 4, y: 4, z: 4, core: 2. Of those that a mesh axis runs over, the one named last changes fastest.
Arguments:
- a_slots: bfloat16 [16, 8, 16, 2, 128, 128], P('grid', 'blk'), may hold values from -6 to 6
- a_rows: int32 [16, 8, 16, 2], P('grid', 'blk'), may hold values from 0 to 127, as said below
- a_cols: int32 [16, 8, 16, 2], P('grid', 'blk'), may hold values from 0 to 63
- a_count: int32 [16, 8, 16], P('grid', 'blk'), may hold values from 0 to 2, as said below
- owned_rows: int32 [16, 8], P('grid'), may hold values from 0 to 127, as said below
- b_matrix: bfloat16 [8192, 8192], P('grid', 'blk'), may hold values from -0.125 to 0.125
Outputs:
- product: bfloat16 [16384, 8192], P('grid', 'blk')
Inputs may be any that keep to these rules, and one draw needn't show every extreme that they name: `a_rows`: every slot sent to product owner g, live or padded, names one of the block rows owned_rows[g, 0 .. 7]; no two slots of the whole draw name the same block row and block column. `a_count`: some product owner receives 2 live slots from every atom owner and atom column. `owned_rows`: A permutation of the 128 block rows.
All inputs are finite; a program needn't handle non-finite values.
Results may differ from a plain program's by a relative error of at most 0.001.
Values may be sent and summed in bfloat16 or wider, within the bound.
A program may use at most 128 MiB of HBM per device.

v0:
```python
import jax
import jax.numpy as jnp
from jax import lax
from jax.sharding import PartitionSpec as P

CAP = 2
RB = 8


def body(a_slots, a_rows, a_cols, a_count, owned_rows, b_matrix):
    groups = lax.axis_size("grid")
    columns = lax.axis_size("blk")
    block_size = a_slots.shape[-1]
    landed = (
        lax.all_to_all(
            a_slots.reshape(groups, CAP, block_size, block_size),
            "grid",
            split_axis=0,
            concat_axis=0,
            tiled=True,
        ),
        lax.all_to_all(
            a_rows.reshape(groups, CAP), "grid", split_axis=0, concat_axis=0, tiled=True
        ),
        lax.all_to_all(
            a_cols.reshape(groups, CAP), "grid", split_axis=0, concat_axis=0, tiled=True
        ),
        lax.all_to_all(a_count.reshape(groups, 1), "grid", split_axis=0, concat_axis=0, tiled=True),
    )
    slot_data, slot_rows, slot_cols, slot_count = (
        lax.all_gather(landed[0][None], "blk", axis=0, tiled=True),
        lax.all_gather(landed[1][None], "blk", axis=0, tiled=True),
        lax.all_gather(landed[2][None], "blk", axis=0, tiled=True),
        lax.all_gather(landed[3][None], "blk", axis=0, tiled=True),
    )
    total = columns * groups * CAP
    live = (jnp.arange(CAP, dtype=jnp.int32)[None, None, :] < slot_count).reshape(total)
    slot_rows = slot_rows.reshape(total)
    slot_cols = slot_cols.reshape(total)
    slot_data = slot_data.reshape(total, block_size, block_size)
    owned = owned_rows.reshape(RB)
    row_hit = (slot_rows[:, None] == owned[None, :]) & live[:, None]
    k_blocks = b_matrix.shape[0] * groups // block_size
    col_hit = slot_cols[:, None] == jnp.arange(k_blocks, dtype=jnp.int32)[None, :]
    placing = (
        (row_hit[:, :, None] & col_hit[:, None, :])
        .reshape(total, RB * k_blocks)
        .astype(jnp.bfloat16)
    )
    spread = jnp.einsum(
        "sp,sq->pq",
        placing,
        slot_data.reshape(total, block_size * block_size),
        preferred_element_type=jnp.float32,
    )
    tile = spread.astype(jnp.bfloat16).reshape(RB, k_blocks, block_size, block_size)
    tile = tile.transpose(0, 2, 1, 3).reshape(RB * block_size, k_blocks * block_size)
    result = jnp.dot(
        tile,
        lax.all_gather(b_matrix, "grid", axis=0, tiled=True),
        preferred_element_type=jnp.float32,
    )
    return result.astype(jnp.bfloat16)


def solution(mesh):
    in_specs = (
        P("grid", "blk", None, None, None, None),
        P("grid", "blk", None, None),
        P("grid", "blk", None, None),
        P("grid", "blk", None),
        P("grid", None),
        P("grid", "blk"),
    )
    out_specs = P("grid", "blk")
    return jax.shard_map(body, mesh=mesh, in_specs=in_specs, out_specs=out_specs, check_vma=False)
```

profile of v0, /device:TPU:1, one launch (start us, length us, event | category | flops | bytes accessed | tf_op | source)
XLA Modules:
  0.0 225.2 jit_solution(14155272657976014603)
XLA Ops:
  6.5 0.0 all-gather.9.cloned.1.call-start
  6.5 24.6 %all_to_all.32 = bf16[16,2,128,128]{3,2,1,0:T(8,128)(2,1)} all-to-all(bf16[16,2,128,128]{3,2,1,0:T(8,128)(2,1)} %bitcast.31), channel_id=1, replica_groups=mesh['grid'=16,'blk'=8] {'grid'}, dimensions={0} | all-to-all | bytes 2097152 | tf_op jit(solution)/shard_map/all_to_all | solution.py:15
  31.1 0.0 all-gather.9.cloned.1.call-update
  31.1 0.0 all-gather.7.cloned.1.call-start
  31.2 0.7 all-gather.7.cloned.1.call-update
  31.9 1.3 copy.15
  33.2 3.6 %all-to-all-start.1 = ((s32[16,1,1]{2,1,0:T(1,128)}), s32[16,1,1]{2,1,0:T(1,128)S(1)}, u32[]{:S(2)}, u32[]{:S(2)}) async-start(s32[16,1,1]{2,1,0:T(1,128)} %copy.15), calls=%async_computation.1 | async-start | bytes 16384 | tf_op jit(solution)/shard_map/all_to_all | solution.py:28
  36.9 1.3 copy.14
  38.2 1.4 copy.16
  39.6 1.3 dynamic-slice
  41.5 1.8 all-to-all-done.1
  43.3 4.9 %all-to-all-start = ((s32[16,1,2]{2,1,0:T(1,128)}), s32[16,1,2]{2,1,0:T(1,128)S(1)}, u32[]{:S(2)}, u32[]{:S(2)}) async-start(s32[16,1,2]{2,1,0:T(1,128)} %copy.14), calls=%async_computation | async-start | bytes 16384 | tf_op jit(solution)/shard_map/all_to_all | solution.py:22
  48.1 0.4 reduce.1
  48.5 0.2 dynamic-update-slice
  48.8 10.3 %all-reduce = s32[128]{0:T(128)S(1)} all-reduce(s32[128]{0:T(128)S(1)} %dynamic-update-slice), channel_id=3, replica_groups=mesh['grid'=16,'blk'=8] {'blk'}, use_global_device_ids=true, to_apply=%add | all-reduce | flops 128 | bytes 1024
  59.1 0.1 lt.23
  59.1 0.1 iota_compare_fusion.1
  59.2 0.1 lt.26
  59.4 0.0 all-to-all-done
  59.4 6.9 %all-to-all-start.2 = ((s32[16,1,2]{2,1,0:T(1,128)}), s32[16,1,2]{2,1,0:T(1,128)S(1)}, u32[]{:S(2)}, u32[]{:S(2)}) async-start(s32[16,1,2]{2,1,0:T(1,128)} %copy.16), calls=%async_computation.2 | async-start | bytes 16384 | tf_op jit(solution)/shard_map/all_to_all | solution.py:25
  66.3 14.7 %all-gather = s32[128,1,2]{2,1,0:T(1,128)S(1)} all-gather(s32[16,1,2]{2,1,0:T(1,128)S(1)} %all-to-all-done), channel_id=2, replica_groups=mesh['grid'=16,'blk'=8] {'blk'}, dimensions={0}, use_global_device_ids=true | all-gather | bytes 1152 | tf_op jit(solution)/shard_map/all_gather | solution.py:32
  81.0 0.6 broadcast.56
  81.6 0.8 reduce.8
  82.5 0.1 eq.40
  82.6 0.0 all-to-all-done.2
  82.6 12.8 %all-gather.2 = s32[128,1,2]{2,1,0:T(1,128)S(1)} all-gather(s32[16,1,2]{2,1,0:T(1,128)S(1)} %all-to-all-done.2), channel_id=4, replica_groups=mesh['grid'=16,'blk'=8] {'blk'}, dimensions={0}, use_global_device_ids=true | all-gather | bytes 1152 | tf_op jit(solution)/shard_map/all_gather | solution.py:33
  95.4 0.9 reduce.7
  96.2 0.1 eq.45
  96.4 0.7 compare_and_fusion
  97.1 0.1 broadcast_and_fusion
  97.2 0.0 all-gather.9.cloned.1.call-done
  97.2 18.5 %fusion.5 = bf16[64,8,128,128]{3,1,2,0:T(8,128)(2,1)} fusion(pred[256,512]{0,1:T(32,128)(4,1)S(1)} %bitcast.32, bf16[32,8,128,128]{3,2,1,0:T(8,128)(2,1)} %bitcast.30), kind=kOutput, calls=%fused_computation.6 | convolution fusion | flops 4303355904 | bytes 25296896 | tf_op jit(solution)/shard_map/sp,sq->pq/dot_general | solution.py:50
  115.7 10.4 %copy.19 = bf16[64,8,128,128]{3,2,1,0:T(8,128)(2,1)S(1)} copy(bf16[64,8,128,128]{3,1,2,0:T(8,128)(2,1)} %fusion.5) | data formatting | bytes 33554432
  126.1 11.8 %copy.17 = bf16[8,64,128,128]{3,1,2,0:T(8,128)(2,1)} copy(bf16[8,64,128,128]{3,2,1,0:T(8,128)(2,1)S(1)} %bitcast.28) | data formatting | bytes 33554432 | tf_op jit(solution)/shard_map/reshape | solution.py:56
  138.0 56.6 %all-gather.7.cloned.1.call-done = bf16[8192,1024]{1,0:T(8,128)(2,1)} async-done(((bf16[512,1024]{1,0:T(8,128)(2,1)}), bf16[8192,1024]{1,0:T(8,128)(2,1)}) %all-gather.7.cloned.1.call-update) | async-done | bytes 16777232 | tf_op jit(solution)/shard_map/all_gather | solution.py:60
  194.6 23.8 %fusion.8 = bf16[1024,1024]{1,0:T(8,128)(2,1)} fusion(bf16[8192,1024]{1,0:T(8,128)(2,1)} %all-gather.7.cloned.1.call-done, bf16[128,8,64,128]{3,2,1,0:T(8,128)(2,1)} %bitcast.29), kind=kOutput, calls=%fused_computation.7 | convolution fusion | flops 17180917760 | bytes 35651584 | tf_op jit(solution)/shard_map/dot_general | solution.py:58
  (2 shorter events, 0.0 us)
Async XLA Ops:
  6.5 90.7 %all-gather.9.cloned.1.call-start = ((), (), s32[]{:S(2)}) async-start(), calls=%async_computation.5 | async-start | bytes 9437184 | tf_op jit(solution)/shard_map/all_gather | solution.py:31
  31.1 163.5 %all-gather.7.cloned.1.call-start = ((), (), s32[]{:S(2)}) async-start(), calls=%async_computation.4 | async-start | bytes 17825792 | tf_op jit(solution)/shard_map/all_gather | solution.py:60
  33.2 10.0 %all-to-all-start.1 = ((s32[16,1,1]{2,1,0:T(1,128)}), s32[16,1,1]{2,1,0:T(1,128)S(1)}, u32[]{:S(2)}, u32[]{:S(2)}) async-start(s32[16,1,1]{2,1,0:T(1,128)} %copy.15), calls=%async_computation.1 | async-start | bytes 16384 | tf_op jit(solution)/shard_map/all_to_all | solution.py:28
  43.3 16.1 %all-to-all-start = ((s32[16,1,2]{2,1,0:T(1,128)}), s32[16,1,2]{2,1,0:T(1,128)S(1)}, u32[]{:S(2)}, u32[]{:S(2)}) async-start(s32[16,1,2]{2,1,0:T(1,128)} %copy.14), calls=%async_computation | async-start | bytes 16384 | tf_op jit(solution)/shard_map/all_to_all | solution.py:22
  59.4 23.2 %all-to-all-start.2 = ((s32[16,1,2]{2,1,0:T(1,128)}), s32[16,1,2]{2,1,0:T(1,128)S(1)}, u32[]{:S(2)}, u32[]{:S(2)}) async-start(s32[16,1,2]{2,1,0:T(1,128)} %copy.16), calls=%async_computation.2 | async-start | bytes 16384 | tf_op jit(solution)/shard_map/all_to_all | solution.py:25
Sparse Core Ops, SparseCore 0:
  31.3 49.8 all-gather.8
  83.3 111.2 all-gather.6
where the time goes:
time: 226 us; the launch traced here: 225 us
  blocking collectives  62.3 us (28%)
  waiting for transfers between devices  59.1 us (26%)
  matrix products  42.3 us (19%)
  local copies, waits for them, and re-layouts  28.9 us (13%)
  starting transfers between devices  15.5 us (7%)
  between operations  14.2 us (6%)
  other arithmetic  2.97 us (1%)
    all_gather x1, waiting for transfers between devices, body(): lax.all_gather(b_matrix, 'grid', axis=0, tiled=True)  56.6 us
    all_to_all x1, blocking collectives, body(): lax.all_to_all(a_slots.reshape(groups, CAP, block_size, block_size), 'gri...  24.6 us
    dot_general x1, matrix products, body(): jnp.dot(tile, lax.all_gather(b_matrix, 'grid', axis=0, tiled=True), prefe...  23.8 us
    dot_general x1, matrix products, body(): jnp.einsum('sp,sq->pq', placing, slot_data.reshape(total, block_size * bl...  18.5 us
    all_gather x1, blocking collectives, body(): lax.all_gather(landed[1][None], 'blk', axis=0, tiled=True)  14.7 us
    all_gather x1, blocking collectives, body(): lax.all_gather(landed[2][None], 'blk', axis=0, tiled=True)  12.8 us
    unnamed x4, local copies, waits for them, and re-layouts  11.9 us
    reshape x1, local copies, waits for them, and re-layouts, body(): spread.astype(jnp.bfloat16).reshape(RB, k_blocks, block_size, block_size)  11.8 us
  transfers between devices with their start and end apart: 5, of which 2 were waited for; matrix products, arithmetic and copies ran while one was open for 22% of the time, Pallas kernels for 0%

commit v1 on v0

--- a/solution.py
+++ b/solution.py
@@ -5,6 +5,29 @@
 
 CAP = 2
 RB = 8
+
+
+def place_the_local_data(u_in, link_axis, on_dim):
+    k_now, w_next, d_next = (
+        lax.axis_size(link_axis),
+        lax.axis_index(link_axis),
+        u_in.shape[on_dim],
+    )
+    table = tuple(((j, (j + 1) % k_now) for j in range(k_now)))
+    rows = tuple(((j, (j - 1) % k_now) for j in range(k_now)))
+    r1 = jnp.zeros((*u_in.shape[:on_dim], k_now * d_next, *u_in.shape[on_dim + 1 :]), u_in.dtype)
+    r1 = lax.dynamic_update_slice_in_dim(r1, u_in, w_next * d_next, axis=on_dim)
+    answer = state_next = u_in
+    main = k_now // 2
+    for t in range(1, main + 1):
+        answer = lax.ppermute(answer, link_axis, table)
+        r1 = lax.dynamic_update_slice_in_dim(r1, answer, (w_next - t) % k_now * d_next, axis=on_dim)
+        if t < k_now - main:
+            state_next = lax.ppermute(state_next, link_axis, rows)
+            r1 = lax.dynamic_update_slice_in_dim(
+                r1, state_next, (w_next + t) % k_now * d_next, axis=on_dim
+            )
+    return r1
 
 
 def body(a_slots, a_rows, a_cols, a_count, owned_rows, b_matrix):
@@ -56,9 +79,7 @@
     tile = spread.astype(jnp.bfloat16).reshape(RB, k_blocks, block_size, block_size)
     tile = tile.transpose(0, 2, 1, 3).reshape(RB * block_size, k_blocks * block_size)
     result = jnp.dot(
-        tile,
-        lax.all_gather(b_matrix, "grid", axis=0, tiled=True),
-        preferred_element_type=jnp.float32,
+        tile, place_the_local_data(b_matrix, "grid", 0), preferred_element_type=jnp.float32
     )
     return result.astype(jnp.bfloat16)
 

time: 226 us -> 410 us (1.81)
  waiting for transfers between devices: 59.1 us -> 125 us
  local copies, waits for them, and re-layouts: 28.9 us -> 88.7 us
  starting transfers between devices: 15.5 us -> 51.3 us
  matrix products: 42.3 us -> 59.1 us
  blocking collectives: 62.3 us -> 67.5 us
    ppermute x0 -> x15, waiting for transfers between devices: none -> 123 us  [the longest x8 104 us: place_the_local_data(): answer = lax.ppermute(answer, link_axis, table)]
    all_gather x1 -> x0, waiting for transfers between devices: 56.6 us -> none  [body(): lax.all_gather(b_matrix, 'grid', axis=0, tiled=True)]
    ppermute x0 -> x15, starting transfers between devices: none -> 34.4 us  [the longest x7 33.8 us: place_the_local_data(): state_next = lax.ppermute(state_next, link_axis, rows)]
    dynamic_update_slice x0 -> x16, local copies, waits for them, and re-layouts: none -> 28 us  [the longest x8 14.6 us: place_the_local_data(): lax.dynamic_update_slice_in_dim(r1, answer, (w_next - t) % k_now * d_next...]
    reshape x1, local copies, waits for them, and re-layouts: 11.8 us -> 37.2 us  [body(): spread.astype(jnp.bfloat16).reshape(RB, k_blocks, block_size, block_size)]
    dot_general x1, matrix products: 23.8 us -> 40.8 us  [body(): jnp.dot(tile, place_the_local_data(b_matrix, 'grid', 0), preferred_elemen...]
    broadcast_in_dim x0 -> x1, local copies, waits for them, and re-layouts: none -> 6 us  [place_the_local_data(): jnp.zeros((*u_in.shape[:on_dim], k_now * d_next, *u_in.shape[on_dim + 1:]...]
    unnamed x1, blocking collectives: 10.3 us -> 15 us
  transfers between devices with their start and end apart: 5 -> 19, of which waited for: 2 -> 9; matrix products, arithmetic and copies ran while one was open for 22% -> 11% of each run, Pallas kernels for 0% -> 0%
where the time goes in v1:
time: 410 us; the launch traced here: 409 us
  waiting for transfers between devices  125 us (30%)
  local copies, waits for them, and re-layouts  88.7 us (22%)
  blocking collectives  67.5 us (16%)
  matrix products  59.1 us (14%)
  starting transfers between devices  51.3 us (13%)
  between operations  14.5 us (4%)
    ppermute x8, waiting for transfers between devices, place_the_local_data(): answer = lax.ppermute(answer, link_axis, table)  104 us
    dot_general x1, matrix products, body(): jnp.dot(tile, place_the_local_data(b_matrix, 'grid', 0), preferred_elemen...  40.8 us
    reshape x1, local copies, waits for them, and re-layouts, body(): spread.astype(jnp.bfloat16).reshape(RB, k_blocks, block_size, block_size)  37.2 us
    ppermute x7, starting transfers between devices, place_the_local_data(): state_next = lax.ppermute(state_next, link_axis, rows)  33.8 us
    all_to_all x1, blocking collectives, body(): lax.all_to_all(a_slots.reshape(groups, CAP, block_size, block_size), 'gri...  24.7 us
    ppermute x7, waiting for transfers between devices, place_the_local_data(): state_next = lax.ppermute(state_next, link_axis, rows)  19.2 us
    dot_general x1, matrix products, body(): jnp.einsum('sp,sq->pq', placing, slot_data.reshape(total, block_size * bl...  18.3 us
    all_gather x1, blocking collectives, body(): lax.all_gather(landed[1][None], 'blk', axis=0, tiled=True)  15.1 us
  transfers between devices with their start and end apart: 19, of which 9 were waited for; matrix products, arithmetic and copies ran while one was open for 11% of the time, Pallas kernels for 0%

profile of v1, /device:TPU:1, one launch (start us, length us, event | category | flops | bytes accessed | tf_op | source)
XLA Modules:
  0.0 408.7 jit_solution(436560443606345604)
XLA Ops:
  6.5 24.7 %all_to_all.32 = bf16[16,2,128,128]{3,2,1,0:T(8,128)(2,1)} all-to-all(bf16[16,2,128,128]{3,2,1,0:T(8,128)(2,1)} %bitcast.31), channel_id=1, replica_groups=mesh['grid'=16,'blk'=8] {'grid'}, dimensions={0} | all-to-all | bytes 2097152 | tf_op jit(solution)/shard_map/all_to_all | solution.py:38
  31.2 0.0 all-gather.6.cloned.1.call-update
  31.3 0.6 collective-permute-start
  31.9 4.2 %collective-permute-start.1 = (bf16[512,1024]{1,0:T(8,128)(2,1)}, bf16[512,1024]{1,0:T(8,128)(2,1)S(1)}, u32[]{:S(2)}, u32[]{:S(2)}) collective-permute-start(bf16[512,1024]{1,0:T(8,128)(2,1)} %param.11), channel_id=1, source_target_pairs={{0,120},{8,0},{16,8},{24,16},{32,24},{40,32},{48,40},{56,48},{64,5... | collective-permute-start | bytes 3145736 | tf_op jit(solution)/shard_map/ppermute | solution.py:26
  36.1 21.5 %collective-permute-done = bf16[512,1024]{1,0:T(8,128)(2,1)S(1)} collective-permute-done((bf16[512,1024]{1,0:T(8,128)(2,1)}, bf16[512,1024]{1,0:T(8,128)(2,1)S(1)}, u32[]{:S(2)}, u32[]{:S(2)}) %collective-permute-start) | collective-permute-done | bytes 1048608 | tf_op jit(solution)/shard_map/ppermute | solution.py:23
  57.6 4.8 %collective-permute-start.3 = (bf16[512,1024]{1,0:T(8,128)(2,1)S(1)}, bf16[512,1024]{1,0:T(8,128)(2,1)S(1)}, u32[]{:S(2)}, u32[]{:S(2)}) collective-permute-start(bf16[512,1024]{1,0:T(8,128)(2,1)S(1)} %collective-permute-done.1), channel_id=1, source_target_pairs={{0,120},{8,0},{16,8},{24,16},{32,24},{40,32},{48,40},{56,48},{64,5... | collective-permute-start | bytes 3145736 | tf_op jit(solution)/shard_map/ppermute | solution.py:26
  62.4 20.3 %collective-permute-done.2 = bf16[512,1024]{1,0:T(8,128)(2,1)S(1)} collective-permute-done((bf16[512,1024]{1,0:T(8,128)(2,1)S(1)}, bf16[512,1024]{1,0:T(8,128)(2,1)S(1)}, u32[]{:S(2)}, u32[]{:S(2)}) %collective-permute-start.2) | collective-permute-done | bytes 1048608 | tf_op jit(solution)/shard_map/ppermute | solution.py:23
  82.7 4.8 %collective-permute-start.5 = (bf16[512,1024]{1,0:T(8,128)(2,1)S(1)}, bf16[512,1024]{1,0:T(8,128)(2,1)S(1)}, u32[]{:S(2)}, u32[]{:S(2)}) collective-permute-start(bf16[512,1024]{1,0:T(8,128)(2,1)S(1)} %collective-permute-done.3), channel_id=1, source_target_pairs={{0,120},{8,0},{16,8},{24,16},{32,24},{40,32},{48,40},{56,48},{64,5... | collective-permute-start | bytes 3145736 | tf_op jit(solution)/shard_map/ppermute | solution.py:26
  87.5 19.4 %collective-permute-done.4 = bf16[512,1024]{1,0:T(8,128)(2,1)S(1)} collective-permute-done((bf16[512,1024]{1,0:T(8,128)(2,1)S(1)}, bf16[512,1024]{1,0:T(8,128)(2,1)S(1)}, u32[]{:S(2)}, u32[]{:S(2)}) %collective-permute-start.4) | collective-permute-done | bytes 1048608 | tf_op jit(solution)/shard_map/ppermute | solution.py:23
  106.9 4.8 %collective-permute-start.7 = (bf16[512,1024]{1,0:T(8,128)(2,1)S(1)}, bf16[512,1024]{1,0:T(8,128)(2,1)}, u32[]{:S(2)}, u32[]{:S(2)}) collective-permute-start(bf16[512,1024]{1,0:T(8,128)(2,1)S(1)} %collective-permute-done.5), channel_id=1, source_target_pairs={{0,120},{8,0},{16,8},{24,16},{32,24},{40,32},{48,40},{56,48},{64,5... | collective-permute-start | bytes 3145736 | tf_op jit(solution)/shard_map/ppermute | solution.py:26
  111.7 18.5 %collective-permute-done.6 = bf16[512,1024]{1,0:T(8,128)(2,1)S(1)} collective-permute-done((bf16[512,1024]{1,0:T(8,128)(2,1)S(1)}, bf16[512,1024]{1,0:T(8,128)(2,1)S(1)}, u32[]{:S(2)}, u32[]{:S(2)}) %collective-permute-start.6) | collective-permute-done | bytes 1048608 | tf_op jit(solution)/shard_map/ppermute | solution.py:23
  130.2 1.0 copy-done.1
  131.2 4.8 %collective-permute-start.9 = (bf16[512,1024]{1,0:T(8,128)(2,1)}, bf16[512,1024]{1,0:T(8,128)(2,1)}, u32[]{:S(2)}, u32[]{:S(2)}) collective-permute-start(bf16[512,1024]{1,0:T(8,128)(2,1)} %collective-permute-done.7), channel_id=1, source_target_pairs={{0,120},{8,0},{16,8},{24,16},{32,24},{40,32},{48,40},{56,48},{64,5... | collective-permute-start | bytes 3145736 | tf_op jit(solution)/shard_map/ppermute | solution.py:26
  136.0 17.7 %collective-permute-done.8 = bf16[512,1024]{1,0:T(8,128)(2,1)} collective-permute-done((bf16[512,1024]{1,0:T(8,128)(2,1)S(1)}, bf16[512,1024]{1,0:T(8,128)(2,1)}, u32[]{:S(2)}, u32[]{:S(2)}) %collective-permute-start.8) | collective-permute-done | bytes 1048608 | tf_op jit(solution)/shard_map/ppermute | solution.py:23
  153.7 1.3 copy.15
  155.0 6.2 %all-to-all-start.1 = ((s32[16,1,1]{2,1,0:T(1,128)}), s32[16,1,1]{2,1,0:T(1,128)S(1)}, u32[]{:S(2)}, u32[]{:S(2)}) async-start(s32[16,1,1]{2,1,0:T(1,128)} %copy.15), calls=%async_computation.1 | async-start | bytes 16384 | tf_op jit(solution)/shard_map/all_to_all | solution.py:51
  161.4 1.4 copy.14
  162.8 1.3 copy.16
  164.1 1.3 dynamic-slice
  165.4 6.0 %broadcast_in_dim.23 = bf16[8192,1024]{1,0:T(8,128)(2,1)} broadcast(bf16[]{:T(256)} %constant.90.clone.1), dimensions={} | broadcast | bytes 16777218 | tf_op jit(solution)/shard_map/broadcast_in_dim | solution.py:18
  171.4 1.0 constant_dynamic-update-slice_fusion.15
  173.1 2.4 all-to-all-done.1
  175.4 4.0 all-to-all-start
  179.5 0.4 reduce.1
  179.9 0.2 dynamic-update-slice
  180.1 15.0 %all-reduce = s32[128]{0:T(128)S(1)} all-reduce(s32[128]{0:T(128)S(1)} %dynamic-update-slice), channel_id=3, replica_groups=mesh['grid'=16,'blk'=8] {'blk'}, use_global_device_ids=true, to_apply=%add | all-reduce | flops 128 | bytes 1024
  195.1 0.1 lt.133
  195.1 0.1 iota_compare_fusion.1
  195.2 0.1 lt.136
  195.4 6.7 %all-to-all-start.2 = ((s32[16,1,2]{2,1,0:T(1,128)}), s32[16,1,2]{2,1,0:T(1,128)S(1)}, u32[]{:S(2)}, u32[]{:S(2)}) async-start(s32[16,1,2]{2,1,0:T(1,128)} %copy.16), calls=%async_computation.2 | async-start | bytes 16384 | tf_op jit(solution)/shard_map/all_to_all | solution.py:48
  202.1 15.1 %all-gather = s32[128,1,2]{2,1,0:T(1,128)S(1)} all-gather(s32[16,1,2]{2,1,0:T(1,128)S(1)} %all-to-all-done), channel_id=2, replica_groups=mesh['grid'=16,'blk'=8] {'blk'}, dimensions={0}, use_global_device_ids=true | all-gather | bytes 1152 | tf_op jit(solution)/shard_map/all_gather | solution.py:55
  217.1 0.6 broadcast.71
  217.7 0.8 reduce.8
  218.6 0.1 eq.56
  218.7 12.8 %all-gather.2 = s32[128,1,2]{2,1,0:T(1,128)S(1)} all-gather(s32[16,1,2]{2,1,0:T(1,128)S(1)} %all-to-all-done.2), channel_id=4, replica_groups=mesh['grid'=16,'blk'=8] {'blk'}, dimensions={0}, use_global_device_ids=true | all-gather | bytes 1152 | tf_op jit(solution)/shard_map/all_gather | solution.py:56
  231.5 0.8 reduce.7
  232.3 0.1 eq.61
  232.5 5.0 %collective-permute-start.11 = (bf16[512,1024]{1,0:T(8,128)(2,1)}, bf16[512,1024]{1,0:T(8,128)(2,1)S(1)}, u32[]{:S(2)}, u32[]{:S(2)}) collective-permute-start(bf16[512,1024]{1,0:T(8,128)(2,1)} %collective-permute-done.9), channel_id=1, source_target_pairs={{0,120},{8,0},{16,8},{24,16},{32,24},{40,32},{48,40},{56,48},{64,5... | collective-permute-start | bytes 3145736 | tf_op jit(solution)/shard_map/ppermute | solution.py:26
  237.5 0.1 compare_and_fusion
  237.6 0.0 collective-permute-start.12
  237.6 0.1 broadcast_and_fusion
  237.7 1.1 constant_dynamic-update-slice_fusion.14
  238.8 1.1 constant_dynamic-update-slice_fusion.13
  239.8 2.3 constant_dynamic-update-slice_fusion.12
  242.1 2.3 constant_dynamic-update-slice_fusion.11
  244.3 2.3 constant_dynamic-update-slice_fusion.10
  246.6 13.6 %collective-permute-done.11 = bf16[512,1024]{1,0:T(8,128)(2,1)S(1)} collective-permute-done((bf16[512,1024]{1,0:T(8,128)(2,1)}, bf16[512,1024]{1,0:T(8,128)(2,1)S(1)}, u32[]{:S(2)}, u32[]{:S(2)}) %collective-permute-start.11) | collective-permute-done | bytes 1048608 | tf_op jit(solution)/shard_map/ppermute | solution.py:26
  260.2 5.4 %collective-permute-start.13 = (bf16[512,1024]{1,0:T(8,128)(2,1)S(1)}, bf16[512,1024]{1,0:T(8,128)(2,1)S(1)}, u32[]{:S(2)}, u32[]{:S(2)}) collective-permute-start(bf16[512,1024]{1,0:T(8,128)(2,1)S(1)} %collective-permute-done.11), channel_id=1, source_target_pairs={{0,120},{8,0},{16,8},{24,16},{32,24},{40,32},{48,40},{56,48},{64,5... | collective-permute-start | bytes 3145736 | tf_op jit(solution)/shard_map/ppermute | solution.py:26
  265.6 2.3 constant_dynamic-update-slice_fusion.9
  267.9 2.3 constant_dynamic-update-slice_fusion.8
  270.3 2.3 constant_dynamic-update-slice_fusion.7
  272.5 2.3 constant_dynamic-update-slice_fusion.6
  274.8 2.3 constant_dynamic-update-slice_fusion.5
  277.1 2.3 constant_dynamic-update-slice_fusion.4
  279.4 1.0 constant_dynamic-update-slice_fusion.3
  280.4 1.1 constant_dynamic-update-slice_fusion.2
  281.5 5.6 %collective-permute-done.13 = bf16[512,1024]{1,0:T(8,128)(2,1)S(1)} collective-permute-done((bf16[512,1024]{1,0:T(8,128)(2,1)S(1)}, bf16[512,1024]{1,0:T(8,128)(2,1)S(1)}, u32[]{:S(2)}, u32[]{:S(2)}) %collective-permute-start.13) | collective-permute-done | bytes 1048608 | tf_op jit(solution)/shard_map/ppermute | solution.py:26
  287.1 1.1 constant_dynamic-update-slice_fusion.1
  288.2 6.4 %collective-permute-done.14 = bf16[512,1024]{1,0:T(8,128)(2,1)S(1)} collective-permute-done((bf16[512,1024]{1,0:T(8,128)(2,1)S(1)}, bf16[512,1024]{1,0:T(8,128)(2,1)S(1)}, u32[]{:S(2)}, u32[]{:S(2)}) %collective-permute-start.14) | collective-permute-done | bytes 1048608 | tf_op jit(solution)/shard_map/ppermute | solution.py:23
  294.6 1.1 constant_dynamic-update-slice_fusion
  295.8 18.3 %fusion.5 = bf16[64,8,128,128]{3,1,2,0:T(8,128)(2,1)} fusion(pred[256,512]{0,1:T(32,128)(4,1)S(1)} %bitcast.32, bf16[32,8,128,128]{3,2,1,0:T(8,128)(2,1)} %bitcast.30), kind=kOutput, calls=%fused_computation.6 | convolution fusion | flops 4303355904 | bytes 25296896 | tf_op jit(solution)/shard_map/sp,sq->pq/dot_general | solution.py:73
  314.1 9.8 %copy.19 = bf16[64,8,128,128]{3,2,1,0:T(8,128)(2,1)S(1)} copy(bf16[64,8,128,128]{3,1,2,0:T(8,128)(2,1)} %fusion.5) | data formatting | bytes 33554432
  323.9 37.2 %copy.17 = bf16[8,64,128,128]{3,1,2,0:T(8,128)(2,1)S(1)} copy(bf16[8,64,128,128]{3,2,1,0:T(8,128)(2,1)S(1)} %bitcast.28) | data formatting | bytes 33554432 | tf_op jit(solution)/shard_map/reshape | solution.py:79
  361.1 40.8 %fusion.8 = bf16[1024,1024]{1,0:T(8,128)(2,1)} fusion(bf16[8192,1024]{1,0:T(8,128)(2,1)} %constant_dynamic-update-slice_fusion, bf16[128,8,64,128]{3,2,1,0:T(8,128)(2,1)S(1)} %bitcast.29), kind=kOutput, calls=%fused_computation.7 | convolution fusion | flops 17180917760 | bytes 35651584 | tf_op jit(solution)/shard_map/dot_general | solution.py:81
  (32 shorter events, 0.1 us)
Async XLA Ops:
  6.5 164.9 %copy-start = (bf16[512,1024]{1,0:T(8,128)(2,1)S(1)}, bf16[512,1024]{1,0:T(8,128)(2,1)}, u32[]{:S(2)}) copy-start(bf16[512,1024]{1,0:T(8,128)(2,1)} %param.11) | copy-start | bytes 3145732
  6.5 231.0 %copy-start.6 = (s32[1,8]{1,0:T(1,128)S(1)}, s32[1,8]{1,0:T(1,128)}, u32[]{:S(2)}) copy-start(s32[1,8]{1,0:T(1,128)} %param.10) | copy-start | bytes 100
  6.5 289.2 %all-gather.6.cloned.1.call-start = ((), (), s32[]{:S(2)}) async-start(), calls=%async_computation.4 | async-start | bytes 9437184 | tf_op jit(solution)/shard_map/all_gather | solution.py:54
  31.3 26.3 %collective-permute-start = (bf16[512,1024]{1,0:T(8,128)(2,1)}, bf16[512,1024]{1,0:T(8,128)(2,1)S(1)}, u32[]{:S(2)}, u32[]{:S(2)}) collective-permute-start(bf16[512,1024]{1,0:T(8,128)(2,1)} %param.11), channel_id=1, source_target_pairs={{0,8},{8,16},{16,24},{24,32},{32,40},{40,48},{48,56},{56,64},{64,7... | collective-permute-start | bytes 3145736 | tf_op jit(solution)/shard_map/ppermute | solution.py:23
  31.9 25.7 %collective-permute-start.1 = (bf16[512,1024]{1,0:T(8,128)(2,1)}, bf16[512,1024]{1,0:T(8,128)(2,1)S(1)}, u32[]{:S(2)}, u32[]{:S(2)}) collective-permute-start(bf16[512,1024]{1,0:T(8,128)(2,1)} %param.11), channel_id=1, source_target_pairs={{0,120},{8,0},{16,8},{24,16},{32,24},{40,32},{48,40},{56,48},{64,5... | collective-permute-start | bytes 3145736 | tf_op jit(solution)/shard_map/ppermute | solution.py:26
  57.6 25.1 %collective-permute-start.2 = (bf16[512,1024]{1,0:T(8,128)(2,1)S(1)}, bf16[512,1024]{1,0:T(8,128)(2,1)S(1)}, u32[]{:S(2)}, u32[]{:S(2)}) collective-permute-start(bf16[512,1024]{1,0:T(8,128)(2,1)S(1)} %collective-permute-done), channel_id=1, source_target_pairs={{0,8},{8,16},{16,24},{24,32},{32,40},{40,48},{48,56},{56,64},{64,7... | collective-permute-start | bytes 3145736 | tf_op jit(solution)/shard_map/ppermute | solution.py:23
  57.6 25.1 %collective-permute-start.3 = (bf16[512,1024]{1,0:T(8,128)(2,1)S(1)}, bf16[512,1024]{1,0:T(8,128)(2,1)S(1)}, u32[]{:S(2)}, u32[]{:S(2)}) collective-permute-start(bf16[512,1024]{1,0:T(8,128)(2,1)S(1)} %collective-permute-done.1), channel_id=1, source_target_pairs={{0,120},{8,0},{16,8},{24,16},{32,24},{40,32},{48,40},{56,48},{64,5... | collective-permute-start | bytes 3145736 | tf_op jit(solution)/shard_map/ppermute | solution.py:26
  82.7 4.8 %copy-start.2 = (bf16[512,1024]{1,0:T(8,128)(2,1)}, bf16[512,1024]{1,0:T(8,128)(2,1)S(1)}, u32[]{:S(2)}) copy-start(bf16[512,1024]{1,0:T(8,128)(2,1)S(1)} %collective-permute-done.2) | copy-start | bytes 3145732
  82.7 24.2 %collective-permute-start.4 = (bf16[512,1024]{1,0:T(8,128)(2,1)S(1)}, bf16[512,1024]{1,0:T(8,128)(2,1)S(1)}, u32[]{:S(2)}, u32[]{:S(2)}) collective-permute-start(bf16[512,1024]{1,0:T(8,128)(2,1)S(1)} %collective-permute-done.2), channel_id=1, source_target_pairs={{0,8},{8,16},{16,24},{24,32},{32,40},{40,48},{48,56},{56,64},{64,7... | collective-permute-start | bytes 3145736 | tf_op jit(solution)/shard_map/ppermute | solution.py:23
  82.7 70.9 %copy-start.4 = (bf16[512,1024]{1,0:T(8,128)(2,1)}, bf16[512,1024]{1,0:T(8,128)(2,1)S(1)}, u32[]{:S(2)}) copy-start(bf16[512,1024]{1,0:T(8,128)(2,1)S(1)} %collective-permute-done.3) | copy-start | bytes 3145732
  82.7 24.2 %collective-permute-start.5 = (bf16[512,1024]{1,0:T(8,128)(2,1)S(1)}, bf16[512,1024]{1,0:T(8,128)(2,1)S(1)}, u32[]{:S(2)}, u32[]{:S(2)}) collective-permute-start(bf16[512,1024]{1,0:T(8,128)(2,1)S(1)} %collective-permute-done.3), channel_id=1, source_target_pairs={{0,120},{8,0},{16,8},{24,16},{32,24},{40,32},{48,40},{56,48},{64,5... | collective-permute-start | bytes 3145736 | tf_op jit(solution)/shard_map/ppermute | solution.py:26
  106.9 46.8 %copy-start.5 = (bf16[512,1024]{1,0:T(8,128)(2,1)}, bf16[512,1024]{1,0:T(8,128)(2,1)S(1)}, u32[]{:S(2)}) copy-start(bf16[512,1024]{1,0:T(8,128)(2,1)S(1)} %collective-permute-done.4) | copy-start | bytes 3145732
  106.9 23.3 %collective-permute-start.6 = (bf16[512,1024]{1,0:T(8,128)(2,1)S(1)}, bf16[512,1024]{1,0:T(8,128)(2,1)S(1)}, u32[]{:S(2)}, u32[]{:S(2)}) collective-permute-start(bf16[512,1024]{1,0:T(8,128)(2,1)S(1)} %collective-permute-done.4), channel_id=1, source_target_pairs={{0,8},{8,16},{16,24},{24,32},{32,40},{40,48},{48,56},{56,64},{64,7... | collective-permute-start | bytes 3145736 | tf_op jit(solution)/shard_map/ppermute | solution.py:23
  106.9 46.7 %copy-start.3 = (bf16[512,1024]{1,0:T(8,128)(2,1)}, bf16[512,1024]{1,0:T(8,128)(2,1)S(1)}, u32[]{:S(2)}) copy-start(bf16[512,1024]{1,0:T(8,128)(2,1)S(1)} %collective-permute-done.5) | copy-start | bytes 3145732
  106.9 24.3 %collective-permute-start.7 = (bf16[512,1024]{1,0:T(8,128)(2,1)S(1)}, bf16[512,1024]{1,0:T(8,128)(2,1)}, u32[]{:S(2)}, u32[]{:S(2)}) collective-permute-start(bf16[512,1024]{1,0:T(8,128)(2,1)S(1)} %collective-permute-done.5), channel_id=1, source_target_pairs={{0,120},{8,0},{16,8},{24,16},{32,24},{40,32},{48,40},{56,48},{64,5... | collective-permute-start | bytes 3145736 | tf_op jit(solution)/shard_map/ppermute | solution.py:26
  130.2 1.0 copy-start.1
  131.2 22.5 %collective-permute-start.8 = (bf16[512,1024]{1,0:T(8,128)(2,1)S(1)}, bf16[512,1024]{1,0:T(8,128)(2,1)}, u32[]{:S(2)}, u32[]{:S(2)}) collective-permute-start(bf16[512,1024]{1,0:T(8,128)(2,1)S(1)} %collective-permute-done.6), channel_id=1, source_target_pairs={{0,8},{8,16},{16,24},{24,32},{32,40},{40,48},{48,56},{56,64},{64,7... | collective-permute-start | bytes 3145736 | tf_op jit(solution)/shard_map/ppermute | solution.py:23
  131.2 101.3 %collective-permute-start.9 = (bf16[512,1024]{1,0:T(8,128)(2,1)}, bf16[512,1024]{1,0:T(8,128)(2,1)}, u32[]{:S(2)}, u32[]{:S(2)}) collective-permute-start(bf16[512,1024]{1,0:T(8,128)(2,1)} %collective-permute-done.7), channel_id=1, source_target_pairs={{0,120},{8,0},{16,8},{24,16},{32,24},{40,32},{48,40},{56,48},{64,5... | collective-permute-start | bytes 3145736 | tf_op jit(solution)/shard_map/ppermute | solution.py:26
  153.7 83.9 %collective-permute-start.10 = (bf16[512,1024]{1,0:T(8,128)(2,1)}, bf16[512,1024]{1,0:T(8,128)(2,1)}, u32[]{:S(2)}, u32[]{:S(2)}) collective-permute-start(bf16[512,1024]{1,0:T(8,128)(2,1)} %collective-permute-done.8), channel_id=1, source_target_pairs={{0,8},{8,16},{16,24},{24,32},{32,40},{40,48},{48,56},{56,64},{64,7... | collective-permute-start | bytes 3145736 | tf_op jit(solution)/shard_map/ppermute | solution.py:23
  155.0 20.4 %all-to-all-start.1 = ((s32[16,1,1]{2,1,0:T(1,128)}), s32[16,1,1]{2,1,0:T(1,128)S(1)}, u32[]{:S(2)}, u32[]{:S(2)}) async-start(s32[16,1,1]{2,1,0:T(1,128)} %copy.15), calls=%async_computation.1 | async-start | bytes 16384 | tf_op jit(solution)/shard_map/all_to_all | solution.py:51
  175.4 20.0 %all-to-all-start = ((s32[16,1,2]{2,1,0:T(1,128)}), s32[16,1,2]{2,1,0:T(1,128)S(1)}, u32[]{:S(2)}, u32[]{:S(2)}) async-start(s32[16,1,2]{2,1,0:T(1,128)} %copy.14), calls=%async_computation | async-start | bytes 16384 | tf_op jit(solution)/shard_map/all_to_all | solution.py:45
  195.4 23.3 %all-to-all-start.2 = ((s32[16,1,2]{2,1,0:T(1,128)}), s32[16,1,2]{2,1,0:T(1,128)S(1)}, u32[]{:S(2)}, u32[]{:S(2)}) async-start(s32[16,1,2]{2,1,0:T(1,128)} %copy.16), calls=%async_computation.2 | async-start | bytes 16384 | tf_op jit(solution)/shard_map/all_to_all | solution.py:48
  232.5 27.7 %collective-permute-start.11 = (bf16[512,1024]{1,0:T(8,128)(2,1)}, bf16[512,1024]{1,0:T(8,128)(2,1)S(1)}, u32[]{:S(2)}, u32[]{:S(2)}) collective-permute-start(bf16[512,1024]{1,0:T(8,128)(2,1)} %collective-permute-done.9), channel_id=1, source_target_pairs={{0,120},{8,0},{16,8},{24,16},{32,24},{40,32},{48,40},{56,48},{64,5... | collective-permute-start | bytes 3145736 | tf_op jit(solution)/shard_map/ppermute | solution.py:26
  237.6 30.3 %collective-permute-start.12 = (bf16[512,1024]{1,0:T(8,128)(2,1)}, bf16[512,1024]{1,0:T(8,128)(2,1)S(1)}, u32[]{:S(2)}, u32[]{:S(2)}) collective-permute-start(bf16[512,1024]{1,0:T(8,128)(2,1)} %collective-permute-done.10), channel_id=1, source_target_pairs={{0,8},{8,16},{16,24},{24,32},{32,40},{40,48},{48,56},{56,64},{64,7... | collective-permute-start | bytes 3145736 | tf_op jit(solution)/shard_map/ppermute | solution.py:23
  260.2 26.9 %collective-permute-start.13 = (bf16[512,1024]{1,0:T(8,128)(2,1)S(1)}, bf16[512,1024]{1,0:T(8,128)(2,1)S(1)}, u32[]{:S(2)}, u32[]{:S(2)}) collective-permute-start(bf16[512,1024]{1,0:T(8,128)(2,1)S(1)} %collective-permute-done.11), channel_id=1, source_target_pairs={{0,120},{8,0},{16,8},{24,16},{32,24},{40,32},{48,40},{56,48},{64,5... | collective-permute-start | bytes 3145736 | tf_op jit(solution)/shard_map/ppermute | solution.py:26
  267.9 26.7 %collective-permute-start.14 = (bf16[512,1024]{1,0:T(8,128)(2,1)S(1)}, bf16[512,1024]{1,0:T(8,128)(2,1)S(1)}, u32[]{:S(2)}, u32[]{:S(2)}) collective-permute-start(bf16[512,1024]{1,0:T(8,128)(2,1)S(1)} %collective-permute-done.12), channel_id=1, source_target_pairs={{0,8},{8,16},{16,24},{24,32},{32,40},{40,48},{48,56},{56,64},{64,7... | collective-permute-start | bytes 3145736 | tf_op jit(solution)/shard_map/ppermute | solution.py:23
Sparse Core Ops, SparseCore 0:
  31.4 49.5 all-gather.5
